TPU v7x, 32 devices: a whole 2x2x4 slice. The times are simulated.
32 devices in a mesh: dp: 8 (over y, x, core), mp: 4 (over z).
Axes of the slice: x: 2, y: 2, z: 4, core: 2. Of those that a mesh axis runs over, the one named last changes fastest.
Arguments:
- layer_input: bfloat16 [6464, 768], P(('dp', 'mp')), may hold values from -6 to 6
- lengths: int32 [32], P('dp'), may hold values from 10 to 202, as said below
- ln1_gain: float32 [768], replicated, may hold values from 0.5 to 1.5
- ln1_bias: float32 [768], replicated, may hold values from -1.25 to 1.25
- w_qkv: bfloat16 [768, 2304], P(None, 'mp'), may hold values from -0.21875 to 0.21875
- b_qkv: float32 [2304], P('mp'), may hold values from -1.25 to 1.25
- features: float32 [12, 64, 32], P('mp'), may hold values from -6 to 6
- w_out: bfloat16 [768, 768], P('mp'), may hold values from -1.75 to 1.75
- b_out: float32 [768], replicated, may hold values from -1.25 to 1.25
- ln2_gain: float32 [768], replicated, may hold values from 0.5 to 1.5
- ln2_bias: float32 [768], replicated, may hold values from -1.25 to 1.25
- w_up: bfloat16 [768, 3072], P(None, 'mp'), may hold values from -0.21875 to 0.21875
- b_up: float32 [3072], P('mp'), may hold values from -1.25 to 1.25
- w_down: bfloat16 [3072, 768], P('mp'), may hold values from -0.109375 to 0.109375
- b_down: float32 [768], replicated, may hold values from -1.25 to 1.25
- cotangent: bfloat16 [6464, 768], P(('dp', 'mp')), may hold values from -6 to 6
Outputs:
- layer_output: bfloat16 [6464, 768], P(('dp', 'mp'))
- grad_x: float32 [6464, 768], P(('dp', 'mp'))
- grad_ln1_gain: float32 [768], replicated
- grad_ln1_bias: float32 [768], replicated
- grad_w_qkv: float32 [768, 2304], P('dp', 'mp')
- grad_b_qkv: float32 [2304], P('mp')
- grad_w_out: float32 [768, 768], P('mp', 'dp')
- grad_b_out: float32 [768], replicated
- grad_ln2_gain: float32 [768], replicated
- grad_ln2_bias: float32 [768], replicated
- grad_w_up: float32 [768, 3072], P('dp', 'mp')
- grad_b_up: float32 [3072], P('mp')
- grad_w_down: float32 [3072, 768], P('mp', 'dp')
- grad_b_down: float32 [768], replicated
Inputs may be any that keep to these rules, and one draw needn't show every extreme that they name: A molecule's live tokens are the first lengths[m] of its 202 slots; some molecule has exactly 202 and some exactly 10.
All inputs are finite; a program needn't handle non-finite values.
Results may differ from a plain program's by a relative error of at most 0.02.
Values may be sent and summed in bfloat16 or wider, within the bound.
A program may use at most 128 MiB of HBM per device.

v0:
```python
import jax
import jax.numpy as jnp
from jax import lax
from jax.sharding import PartitionSpec as P

MAXLEN = 202
EPSILON = 1e-05


def norm_rows(values, gain, shift):
    centred = values - jnp.mean(values, axis=-1, keepdims=True)
    factor = lax.rsqrt(jnp.mean(centred * centred, axis=-1, keepdims=True) + EPSILON)
    normed = centred * factor
    return (normed * gain + shift, normed, factor)


def norm_back(grad_norm, normed, factor, gain):
    grad_hat = grad_norm * gain
    inner = (
        grad_hat
        - jnp.mean(grad_hat, axis=-1, keepdims=True)
        - normed * jnp.mean(grad_hat * normed, axis=-1, keepdims=True)
    )
    return (factor * inner, jnp.sum(grad_norm * normed, axis=0), jnp.sum(grad_norm, axis=0))


def rotate(values, positions):
    half = values.shape[-1] // 2
    freq = 10000.0 ** (-jnp.arange(half, dtype=jnp.float32) * 2.0 / values.shape[-1])
    angle = positions.astype(jnp.float32)[:, None] * freq[None, :]
    cosine = jnp.concatenate([jnp.cos(angle), jnp.cos(angle)], axis=-1)[:, None, :]
    sine = jnp.concatenate([jnp.sin(angle), jnp.sin(angle)], axis=-1)[:, None, :]
    turned = jnp.concatenate([-values[..., half:], values[..., :half]], axis=-1)
    return values * cosine + turned * sine


def featurize(projected, features, positions):
    heads = features.shape[0]
    head_size = features.shape[1]
    blocks = projected.reshape(projected.shape[0], heads, 3, head_size)
    factor = head_size ** (-0.25)
    query = rotate(blocks[:, :, 0], positions) * factor
    keyed = rotate(blocks[:, :, 1], positions) * factor
    map_q = (
        jax.nn.elu(jnp.einsum("ghe,hef->ghf", query, features, precision=lax.Precision.HIGHEST))
        + 1.0
    )
    map_k = (
        jax.nn.elu(jnp.einsum("ghe,hef->ghf", keyed, features, precision=lax.Precision.HIGHEST))
        + 1.0
    )
    return (map_q, map_k, blocks[:, :, 2])


def core(map_q, map_k, column_block, key_mask, molecules):
    total_rows, heads, feats = map_q.shape
    head_size = column_block.shape[-1]
    span = total_rows // molecules
    query_maps = map_q.reshape(molecules, span, heads, feats)
    key_maps = (map_k * key_mask[:, None, None]).reshape(molecules, span, heads, feats)
    values_four = column_block.reshape(molecules, span, heads, head_size)
    state = jnp.einsum("mlhf,mlhe->mhfe", key_maps, values_four, precision=lax.Precision.HIGHEST)
    summed = jnp.sum(key_maps, axis=1)
    numer = jnp.einsum("mlhf,mhfe->mlhe", query_maps, state, precision=lax.Precision.HIGHEST)
    denom = jnp.einsum("mlhf,mhf->mlh", query_maps, summed, precision=lax.Precision.HIGHEST)
    return (numer / denom[..., None]).reshape(total_rows, heads * head_size)


def gelu_exact(argument):
    return jax.nn.gelu(argument, approximate=False)


def contract_last(left, right):
    return lax.dot_general(
        left, right, (((1,), (1,)), ((), ())), preferred_element_type=jnp.float32
    )


def contract_first(left, right):
    return lax.dot_general(
        left, right, (((0,), (0,)), ((), ())), preferred_element_type=jnp.float32
    )


def slot_masks(counts):
    slot_index = jnp.arange(MAXLEN, dtype=jnp.int32)
    number = counts.shape[0]
    mask_rows = (slot_index[None, :] < counts[:, None]).astype(jnp.float32).reshape(number * MAXLEN)
    return (mask_rows, jnp.tile(slot_index, number))


def local(
    layer_input,
    lengths,
    ln1_gain,
    ln1_bias,
    w_qkv,
    b_qkv,
    features,
    w_out,
    b_out,
    ln2_gain,
    ln2_bias,
    w_up,
    b_up,
    w_down,
    b_down,
    cotangent,
):
    inputs = layer_input.astype(jnp.float32)
    normed_one, hat_one, factor_one = norm_rows(inputs, ln1_gain, ln1_bias)
    first_local = normed_one.astype(jnp.bfloat16)
    qkv_matrix, out_matrix, qkv_bias, feature_set = (w_qkv, w_out, b_qkv, features)
    attn_mask, attn_positions = slot_masks(lengths)
    attn_molecules = lengths.shape[0]
    first_rows = lax.all_gather(first_local, "mp", axis=0, tiled=True)
    projected = jnp.dot(first_rows, qkv_matrix, preferred_element_type=jnp.float32) + qkv_bias
    feature_out, feature_pull = jax.vjp(
        lambda argument: featurize(argument, feature_set, attn_positions), projected
    )
    widened = tuple((member.astype(jnp.bfloat16).astype(jnp.float32) for member in feature_out))
    attended, core_pull = jax.vjp(
        lambda query_map, key_map, column_block: core(
            query_map, key_map, column_block, attn_mask, attn_molecules
        ),
        *widened
    )
    mixed = attended.astype(jnp.bfloat16)
    middle = (
        inputs
        + lax.psum_scatter(
            jnp.dot(mixed, w_out, preferred_element_type=jnp.float32).astype(jnp.bfloat16),
            "mp",
            scatter_dimension=0,
            tiled=True,
        ).astype(jnp.float32)
        + b_out
    )
    normed_two, hat_two, factor_two = norm_rows(middle, ln2_gain, ln2_bias)
    second = normed_two.astype(jnp.bfloat16)
    second_rows = lax.all_gather(second, "mp", axis=0, tiled=True)
    pre_act = jnp.dot(second_rows, w_up, preferred_element_type=jnp.float32) + b_up
    activated, gelu_pull = jax.vjp(gelu_exact, pre_act)
    hidden = activated.astype(jnp.bfloat16)
    ffn_branch = (
        lax.psum_scatter(
            jnp.dot(hidden, w_down, preferred_element_type=jnp.float32).astype(jnp.bfloat16),
            "mp",
            scatter_dimension=0,
            tiled=True,
        ).astype(jnp.float32)
        + b_down
    )
    outputs = (middle + ffn_branch).astype(jnp.bfloat16)
    grad_output = cotangent.astype(jnp.float32)
    grad_b_down = jnp.sum(grad_output, axis=0)
    grad_rows = lax.all_gather(cotangent, "mp", axis=0, tiled=True)
    grad_hidden = contract_last(grad_rows, w_down)
    grad_pre = gelu_pull(grad_hidden)[0].astype(jnp.bfloat16)
    grad_w_down = contract_first(hidden, grad_rows)
    grad_w_up = contract_first(second_rows, grad_pre)
    grad_b_up = jnp.sum(grad_pre.astype(jnp.float32), axis=0)
    grad_second = lax.psum_scatter(
        contract_last(grad_pre, w_up).astype(jnp.bfloat16), "mp", scatter_dimension=0, tiled=True
    ).astype(jnp.float32)
    grad_mid_norm, grad_ln2_gain, grad_ln2_bias = norm_back(
        grad_second, hat_two, factor_two, ln2_gain
    )
    grad_middle = grad_output + grad_mid_norm
    grad_branch = grad_middle.astype(jnp.bfloat16)
    grad_b_out = jnp.sum(grad_branch.astype(jnp.float32), axis=0)
    branch_rows = lax.all_gather(grad_branch, "mp", axis=0, tiled=True)
    grad_mixed = contract_last(branch_rows, out_matrix)
    out_part = contract_first(mixed, branch_rows)
    grad_maps = core_pull(grad_mixed)
    grad_projected = feature_pull(grad_maps)[0].astype(jnp.bfloat16)
    qkv_bias_part = jnp.sum(grad_projected.astype(jnp.float32), axis=0)
    qkv_part = contract_first(first_rows, grad_projected)
    grad_w_qkv, grad_b_qkv, grad_w_out = (qkv_part, qkv_bias_part, out_part)
    grad_first = lax.psum_scatter(
        contract_last(grad_projected, w_qkv).astype(jnp.bfloat16),
        "mp",
        scatter_dimension=0,
        tiled=True,
    ).astype(jnp.float32)
    grad_in_norm, grad_ln1_gain, grad_ln1_bias = norm_back(
        grad_first, hat_one, factor_one, ln1_gain
    )
    grad_inputs = grad_middle + grad_in_norm
    grad_w_qkv, grad_w_out, grad_w_up, grad_w_down = (
        lax.psum_scatter(grad_w_qkv, "dp", scatter_dimension=0, tiled=True),
        lax.psum_scatter(grad_w_out, "dp", scatter_dimension=1, tiled=True),
        lax.psum_scatter(grad_w_up, "dp", scatter_dimension=0, tiled=True),
        lax.psum_scatter(grad_w_down, "dp", scatter_dimension=1, tiled=True),
    )
    grad_b_qkv, grad_b_up = lax.psum((grad_b_qkv, grad_b_up), "dp")
    summed_small = lax.psum(
        (grad_ln1_gain, grad_ln1_bias, grad_b_out, grad_ln2_gain, grad_ln2_bias, grad_b_down),
        ("dp", "mp"),
    )
    return (
        outputs,
        grad_inputs,
        summed_small[0],
        summed_small[1],
        grad_w_qkv,
        grad_b_qkv,
        grad_w_out,
        summed_small[2],
        summed_small[3],
        summed_small[4],
        grad_w_up,
        grad_b_up,
        grad_w_down,
        summed_small[5],
    )


def solution(mesh):
    placed = (
        P(("dp", "mp"), None),
        P("dp"),
        P(),
        P(),
        P(None, "mp"),
        P("mp"),
        P("mp", None, None),
        P("mp", None),
        P(),
        P(),
        P(),
        P(None, "mp"),
        P("mp"),
        P("mp", None),
        P(),
        P(("dp", "mp"), None),
    )
    return jax.shard_map(
        local,
        mesh=mesh,
        in_specs=placed,
        out_specs=(
            P(("dp", "mp"), None),
            P(("dp", "mp"), None),
            P(),
            P(),
            P("dp", "mp"),
            P("mp"),
            P("mp", "dp"),
            P(),
            P(),
            P(),
            P("dp", "mp"),
            P("mp"),
            P("mp", "dp"),
            P(),
        ),
        check_vma=False,
    )
```

profile of v0, /device:TPU:0, one launch (start us, length us, event | category | flops | bytes accessed | tf_op | source)
XLA Modules:
  0.0 409.1 jit_solution(9099996804335391851)
XLA Ops:
  14.7 31.8 %all-gather.9.cloned.1.call-done = bf16[4,202,768]{2,1,0:T(8,128)(2,1)} async-done(((bf16[1,202,768]{2,1,0:T(8,128)(2,1)}), bf16[4,202,768]{2,1,0:T(8,128)(2,1)}) %all-gather.9.cloned.1.call-update) | async-done | bytes 1241104 | tf_op jit(solution)/shard_map/all_gather | solution.py:116
  48.1 2.7 convolution_add_fusion
  63.6 2.4 divide_convert_fusion
  68.3 32.9 %fusion = bf16[208,768]{1,0:T(8,128)(2,1)} fusion(bf16[808,768]{1,0:T(8,128)(2,1)S(1)} %convolution_convert_fusion.2), kind=kCustom, calls=%all-reduce-scatter | all-reduce-scatter fusion | flops 638977 | bytes 1561088
  109.4 2.7 reshape.158
  112.1 30.2 %all-gather.11.cloned.1.call-done = bf16[4,202,768]{2,1,0:T(8,128)(2,1)} async-done(((bf16[1,202,768]{2,1,0:T(8,128)(2,1)}), bf16[4,202,768]{2,1,0:T(8,128)(2,1)}) %all-gather.11.cloned.1.call-update) | async-done | bytes 1241104 | tf_op jit(solution)/shard_map/all_gather | solution.py:141
  144.0 2.9 fusion.115
  146.9 8.4 %convert_reduce_fusion = (f32[768]{0:T(1024)}, bf16[808,768]{1,0:T(8,128)(2,1)S(1)}, f32[808,768]{1,0:T(8,128)}) fusion(f32[808,768]{1,0:T(8,128)S(1)} %fusion.115, f32[768]{0:T(1024)S(1)} %copy-done.41, bf16[808,768]{1,0:T(8,128)(2,1)S(1)} %copy-done.13, bf16[768,768]{1,0:T(8,128)(2,1)S(1)} %copy-done), kind=kOutput, calls=%fused_computation.2 | convolution fusion | flops 999695616 | bytes 8632320 | tf_op jit(solution)/shard_map/dot_general | solution.py:74
  156.4 2.3 convolution_convert_fusion
  158.7 28.5 %fusion.2 = bf16[208,768]{1,0:T(8,128)(2,1)S(1)} fusion(bf16[808,768]{1,0:T(8,128)(2,1)} %convolution_convert_fusion), kind=kCustom, calls=%all-reduce-scatter.2 | all-reduce-scatter fusion | flops 638977 | bytes 1561088
  195.1 31.9 %all-gather.15.cloned.1.call-done = bf16[4,202,768]{2,1,0:T(8,128)(2,1)} async-done(((bf16[1,202,768]{2,1,0:T(8,128)(2,1)}), bf16[4,202,768]{2,1,0:T(8,128)(2,1)}) %all-gather.15.cloned.1.call-update) | async-done | bytes 1241104 | tf_op jit(solution)/shard_map/all_gather | solution.py:172
  228.7 2.6 convolution_bitcast_fusion
  231.4 2.9 multiply_convert_fusion
  235.4 2.9 fusion.119
  240.5 4.6 %fusion.118 = f32[768,768]{1,0:T(8,128)} fusion(bf16[808,768]{1,0:T(8,128)(2,1)} %copy-done.12, bf16[808,768]{1,0:T(8,128)(2,1)} %copy-done.47), kind=kOutput, calls=%fused_computation.196 | convolution fusion | flops 953155584 | bytes 4841472 | tf_op jit(solution)/shard_map/dot_general | solution.py:80
  245.4 2.5 fusion.116
  268.5 2.7 fusion.117
  273.5 2.3 convolution_convert_fusion.3
  275.8 47.7 %fusion.110 = (bf16[208,768]{1,0:T(8,128)(2,1)S(1)}, bf16[208,768]{1,0:T(8,128)(2,1)S(1)}) fusion(bf16[808,768]{1,0:T(8,128)(2,1)} %convolution_convert_fusion.1, bf16[808,768]{1,0:T(8,128)(2,1)} %convolution_convert_fusion.3), kind=kCustom, calls=%all-reduce-scatter.4 | all-reduce-scatter fusion | flops 1277953 | bytes 3121664
  323.6 2.6 collective-permute-start.3
  326.8 2.6 collective-permute-start.1
  329.6 13.6 %all-reduce.16 = (f32[576]{0:T(1024)}, f32[768]{0:T(1024)}) all-reduce(f32[576]{0:T(1024)S(1)} %reduce_sum.181, f32[768]{0:T(1024)S(1)} %copy-done.42), channel_id=1, replica_groups=mesh['dp'=8,'mp'=4] {'dp'}, use_global_device_ids=true, to_apply=%region_20.21 | all-reduce | flops 1344 | bytes 10752 | tf_op jit(solution)/shard_map/psum | solution.py:196
  345.2 38.1 %all-reduce.15 = (f32[768]{0:T(1024)}, f32[768]{0:T(1024)}, f32[768]{0:T(1024)}, f32[768]{0:T(1024)}, f32[768]{0:T(1024)}, /*index=5*/f32[768]{0:T(1024)}) all-reduce(f32[768]{0:T(1024)S(1)} %get-tuple-element.16, f32[768]{0:T(1024)S(1)} %get-tuple-element.21, ...), channel_id=1, replica_groups=mesh['dp'=8,'mp'=4] {'dp','mp'}, use_global_device_ids=true, to_apply=%region_15.16 | all-reduce | flops 4608 | bytes 36864 | tf_op jit(solution)/shard_map/psum | solution.py:197
  387.1 15.2 %reduce-scatter.15.cloned.1.call-done = f32[96,576]{1,0:T(8,128)} async-done(((f32[768,576]{1,0:T(8,128)}), f32[96,576]{1,0:T(8,128)}) %reduce-scatter.15.cloned.1.call-update) | async-done | bytes 221200 | tf_op jit(solution)/shard_map/reduce_scatter | solution.py:191
  (208 shorter events, 76.4 us)
Async XLA Ops:
  7.2 139.7 %copy-start = (bf16[768,768]{1,0:T(8,128)(2,1)S(1)}, bf16[768,768]{1,0:T(8,128)(2,1)}, u32[]{:S(2)}) copy-start(bf16[768,768]{1,0:T(8,128)(2,1)} %param.29) | copy-start | bytes 3538948
  7.2 39.3 %all-gather.9.cloned.1.call-start = ((), (), s32[]{:S(2)}) async-start(), calls=%async_computation.7 | async-start | bytes 1597440 | tf_op jit(solution)/shard_map/all_gather | solution.py:116
  9.7 38.5 %copy-start.46 = (f32[576]{0:T(1024)S(1)}, f32[576]{0:T(1024)}, u32[]{:S(2)}) copy-start(f32[576]{0:T(1024)} %param.21) | copy-start | bytes 6916
  11.7 97.7 %all-gather.13.cloned.1.call-start = ((), (), s32[]{:S(2)}) async-start(), calls=%async_computation.9 | async-start | bytes 1597440 | tf_op jit(solution)/shard_map/all_gather | solution.py:157
  12.4 129.9 %all-gather.11.cloned.1.call-start = ((), (), s32[]{:S(2)}) async-start(), calls=%async_computation.8 | async-start | bytes 1597440 | tf_op jit(solution)/shard_map/all_gather | solution.py:141
  13.3 45.4 %copy-start.27 = (f32[808]{0:T(1024)}, f32[808]{0:T(1024)S(1)}, u32[]{:S(2)}) copy-start(f32[808]{0:T(1024)S(1)} %reshape.152) | copy-start | bytes 9700
  66.3 40.5 %copy-start.1 = (bf16[202,768]{1,0:T(8,128)(2,1)S(1)}, bf16[202,768]{1,0:T(8,128)(2,1)}, u32[]{:S(2)}) copy-start(bf16[202,768]{1,0:T(8,128)(2,1)} %param.16) | copy-start | bytes 930820
  66.3 40.5 %copy-start.24 = (f32[768]{0:T(1024)S(1)}, f32[768]{0:T(1024)}, u32[]{:S(2)}) copy-start(f32[768]{0:T(1024)} %param.24) | copy-start | bytes 9220
  66.6 37.8 %copy-start.6 = (bf16[808,192]{0,1:T(8,128)(2,1)}, bf16[808,192]{0,1:T(8,128)(2,1)S(1)}, u32[]{:S(2)}) copy-start(bf16[808,192]{0,1:T(8,128)(2,1)S(1)} %convert_element_type.131) | copy-start | bytes 930820
  101.9 2.9 collective-permute-start
  109.1 117.9 %all-gather.15.cloned.1.call-start = ((), (), s32[]{:S(2)}) async-start(), calls=%async_computation.10 | async-start | bytes 1597440 | tf_op jit(solution)/shard_map/all_gather | solution.py:172
  187.3 3.2 collective-permute-start.2
  195.0 190.4 %reduce-scatter.21.cloned.1.call-start = ((), (), s32[]{:S(2)}) async-start(), calls=%async_computation.11 | async-start | bytes 884736
  231.3 155.8 %reduce-scatter.19.cloned.1.call-start = ((), (), s32[]{:S(2)}) async-start(), calls=%async_computation.6 | async-start | bytes 2654208 | tf_op jit(solution)/shard_map/reduce_scatter | solution.py:194
  238.3 148.8 %reduce-scatter.17.cloned.1.call-start = ((), (), s32[]{:S(2)}) async-start(), calls=%async_computation.5 | async-start | bytes 2654208 | tf_op jit(solution)/shard_map/reduce_scatter | solution.py:193
  245.1 157.2 %reduce-scatter.15.cloned.1.call-start = ((), (), s32[]{:S(2)}) async-start(), calls=%async_computation.4 | async-start | bytes 2211840 | tf_op jit(solution)/shard_map/reduce_scatter | solution.py:191
  275.8 53.8 %copy-start.42 = (f32[768]{0:T(1024)S(1)}, f32[768]{0:T(1024)}, u32[]{:S(2)}) copy-start(f32[768]{0:T(1024)} %get-tuple-element.34) | copy-start | bytes 9220
  275.8 68.9 %copy-start.26 = (f32[768]{0:T(1024)S(1)}, f32[768]{0:T(1024)}, u32[]{:S(2)}) copy-start(f32[768]{0:T(1024)} %param.18) | copy-start | bytes 9220
  275.8 68.9 %copy-start.30 = (f32[202]{0:T(256)S(1)}, f32[202]{0:T(256)}, u32[]{:S(2)}) copy-start(f32[202]{0:T(256)} %copy-done.29) | copy-start | bytes 2428
  275.8 68.9 %copy-start.34 = (f32[202]{0:T(256)S(1)}, f32[202]{0:T(256)}, u32[]{:S(2)}) copy-start(f32[202]{0:T(256)} %copy-done.33) | copy-start | bytes 2428
  275.8 69.4 %copy-start.35 = (f32[768]{0:T(1024)S(1)}, f32[768]{0:T(1024)}, u32[]{:S(2)}) copy-start(f32[768]{0:T(1024)} %get-tuple-element.14) | copy-start | bytes 9220
  275.8 107.5 %copy-start.3 = (f32[202,768]{1,0:T(8,128)S(1)}, f32[202,768]{1,0:T(8,128)}, u32[]{:S(2)}) copy-start(f32[202,768]{1,0:T(8,128)} %copy-done.2) | copy-start | bytes 1861636
  323.6 19.5 %collective-permute-start.3 = (bf16[18,768]{1,0:T(8,128)(2,1)S(1)}, bf16[18,768]{1,0:T(8,128)(2,1)S(1)}, u32[]{:S(2)}, u32[]{:S(2)}) collective-permute-start(bf16[18,768]{1,0:T(8,128)(2,1)S(1)} %slice.39), channel_id=1, source_target_pairs={{0,1},{1,2},{2,3},{4,5},{5,6},{6,7},{8,9},{9,10},{10,11},{12,13},{... | collective-permute-start | bytes 82952
  326.8 16.7 %collective-permute-start.1 = (bf16[18,768]{1,0:T(8,128)(2,1)}, bf16[18,768]{1,0:T(8,128)(2,1)}, u32[]{:S(2)}, u32[]{:S(2)}) collective-permute-start(bf16[18,768]{1,0:T(8,128)(2,1)} %slice.37), channel_id=1, source_target_pairs={{0,1},{1,2},{2,3},{4,5},{5,6},{6,7},{8,9},{9,10},{10,11},{12,13},{... | collective-permute-start | bytes 82952
  (36 other events, 253.7 us)
Sparse Core Ops, SparseCore 0:
  11.8 34.6 all-gather.8
  48.1 36.3 all-gather.12
  109.2 33.0 all-gather.10
  195.1 31.8 all-gather.14
  231.4 34.0 reduce-scatter.20
  269.3 42.3 reduce-scatter.18
  315.6 42.4 reduce-scatter.16
  362.1 40.1 reduce-scatter.14
where the time goes:
time: 411 us; the launch traced here: 409 us
  blocking collectives  161 us (39%)
  waiting for transfers between devices  112 us (27%)
  matrix products  54.1 us (13%)
  local copies, waits for them, and re-layouts  35.5 us (9%)
  other arithmetic  22.2 us (5%)
  between operations  15.7 us (4%)
  starting transfers between devices  8.88 us (2%)
    unnamed x3, blocking collectives  109 us
    psum x1, blocking collectives, local(): lax.psum((grad_ln1_gain, grad_ln1_bias, grad_b_out, grad_ln2_gain, grad_l...  38.1 us
    all_gather x1, waiting for transfers between devices, local(): branch_rows = lax.all_gather(grad_branch, 'mp', axis=0, tiled=True)  31.9 us
    all_gather x1, waiting for transfers between devices, local(): first_rows = lax.all_gather(first_local, 'mp', axis=0, tiled=True)  31.8 us
    all_gather x1, waiting for transfers between devices, local(): second_rows = lax.all_gather(second, 'mp', axis=0, tiled=True)  30.2 us
    unnamed x111, local copies, waits for them, and re-layouts  20.4 us
    dot_general x4, matrix products, contract_last(): lax.dot_general(left, right, (((1,), (1,)), ((), ())), preferred_element_...  15.5 us
    reduce_scatter x1, waiting for transfers between devices, local(): lax.psum_scatter(grad_w_qkv, 'dp', scatter_dimension=0, tiled=True)  15.2 us
  transfers between devices with their start and end apart: 12, of which 6 were waited for; matrix products, arithmetic and copies ran while one was open for 39% of the time, Pallas kernels for 0%

commit v1 on v0

--- a/solution.py
+++ b/solution.py
@@ -2,9 +2,34 @@
 import jax.numpy as jnp
 from jax import lax
 from jax.sharding import PartitionSpec as P
+from jax.lax import axis_index, axis_size, ppermute
 
 MAXLEN = 202
 EPSILON = 1e-05
+
+
+def _build_loads(u_in, in_dim):
+    u_in = jnp.moveaxis(u_in, 0, in_dim)
+    k_now = u_in.shape
+    known = u_in.reshape(*k_now[:in_dim], k_now[in_dim] * k_now[in_dim + 1], *k_now[in_dim + 2 :])
+    return known
+
+
+def part_the_routes_all(work_x, chip_axis):
+    q_next, newest = (axis_size(chip_axis), axis_index(chip_axis))
+    frame_out, current_value = (work_x[None], 1)
+    while current_value < q_next:
+        all_rows = ppermute(
+            frame_out,
+            axis_name=chip_axis,
+            perm=tuple(((t, t ^ current_value) for t in range(q_next))),
+        )
+        x_next = newest & current_value == 0
+        frame_out = jnp.concatenate(
+            [jnp.where(x_next, frame_out, all_rows), jnp.where(x_next, all_rows, frame_out)]
+        )
+        current_value *= 2
+    return frame_out
 
 
 def norm_rows(values, gain, shift):
@@ -169,7 +194,7 @@
     grad_middle = grad_output + grad_mid_norm
     grad_branch = grad_middle.astype(jnp.bfloat16)
     grad_b_out = jnp.sum(grad_branch.astype(jnp.float32), axis=0)
-    branch_rows = lax.all_gather(grad_branch, "mp", axis=0, tiled=True)
+    branch_rows = _build_loads(part_the_routes_all(grad_branch, "mp"), 0)
     grad_mixed = contract_last(branch_rows, out_matrix)
     out_part = contract_first(mixed, branch_rows)
     grad_maps = core_pull(grad_mixed)

time: 411 us -> 418 us (1.017)
    all_gather x1 -> x0, waiting for transfers between devices: 31.9 us -> none  [local(): branch_rows = lax.all_gather(grad_branch, 'mp', axis=0, tiled=True)]
    ppermute x0 -> x2, waiting for transfers between devices: none -> 30.8 us  [part_the_routes_all(): ppermute(frame_out, axis_name=chip_axis, perm=tuple(((t, t ^ current_valu...]
    unnamed x111 -> x116, local copies, waits for them, and re-layouts: 20.4 us -> 20.7 us
  transfers between devices with their start and end apart: 12 -> 13, of which waited for: 6 -> 7; matrix products, arithmetic and copies ran while one was open for 39% -> 37% of each run, Pallas kernels for 0% -> 0%
where the time goes in v1:
time: 418 us; the launch traced here: 417 us
  blocking collectives  162 us (39%)
  waiting for transfers between devices  114 us (27%)
  matrix products  52.4 us (13%)
  local copies, waits for them, and re-layouts  36.8 us (9%)
  other arithmetic  23.8 us (6%)
  between operations  15.7 us (4%)
  starting transfers between devices  12.2 us (3%)
    unnamed x3, blocking collectives  110 us
    psum x1, blocking collectives, local(): lax.psum((grad_ln1_gain, grad_ln1_bias, grad_b_out, grad_ln2_gain, grad_l...  38.2 us
    all_gather x1, waiting for transfers between devices, local(): first_rows = lax.all_gather(first_local, 'mp', axis=0, tiled=True)  31.8 us
    ppermute x2, waiting for transfers between devices, part_the_routes_all(): ppermute(frame_out, axis_name=chip_axis, perm=tuple(((t, t ^ current_valu...  30.8 us
    all_gather x1, waiting for transfers between devices, local(): second_rows = lax.all_gather(second, 'mp', axis=0, tiled=True)  30.3 us
    unnamed x116, local copies, waits for them, and re-layouts  20.7 us
    reduce_scatter x1, waiting for transfers between devices, local(): lax.psum_scatter(grad_w_qkv, 'dp', scatter_dimension=0, tiled=True)  18.7 us
    dot_general x4, matrix products, contract_last(): lax.dot_general(left, right, (((1,), (1,)), ((), ())), preferred_element_...  14.9 us
  transfers between devices with their start and end apart: 13, of which 7 were waited for; matrix products, arithmetic and copies ran while one was open for 37% of the time, Pallas kernels for 0%

profile of v1, /device:TPU:0, one launch (start us, length us, event | category | flops | bytes accessed | tf_op | source)
XLA Modules:
  0.0 417.0 jit_solution(10652201061867154993)
XLA Ops:
  14.7 31.8 %all-gather.7.cloned.1.call-done = bf16[4,202,768]{2,1,0:T(8,128)(2,1)} async-done(((bf16[1,202,768]{2,1,0:T(8,128)(2,1)}), bf16[4,202,768]{2,1,0:T(8,128)(2,1)}) %all-gather.7.cloned.1.call-update) | async-done | bytes 1241104 | tf_op jit(solution)/shard_map/all_gather | solution.py:141
  46.5 2.7 reshape.159
  49.2 2.7 convolution_add_fusion
  66.7 33.8 %fusion = bf16[208,768]{1,0:T(8,128)(2,1)S(1)} fusion(bf16[808,768]{1,0:T(8,128)(2,1)} %convolution_convert_fusion.2), kind=kCustom, calls=%all-reduce-scatter | all-reduce-scatter fusion | flops 638977 | bytes 1561088
  105.7 2.7 reshape.163
  108.4 30.3 %all-gather.9.cloned.1.call-done = bf16[4,202,768]{2,1,0:T(8,128)(2,1)} async-done(((bf16[1,202,768]{2,1,0:T(8,128)(2,1)}), bf16[4,202,768]{2,1,0:T(8,128)(2,1)}) %all-gather.9.cloned.1.call-update) | async-done | bytes 1241104 | tf_op jit(solution)/shard_map/all_gather | solution.py:166
  138.6 2.8 reshape.161
  141.4 2.9 fusion.115
  144.4 8.4 %convert_reduce_fusion = (f32[768]{0:T(1024)}, bf16[808,768]{1,0:T(8,128)(2,1)S(1)}, f32[808,768]{1,0:T(8,128)}) fusion(f32[808,768]{1,0:T(8,128)S(1)} %fusion.115, f32[768]{0:T(1024)S(1)} %copy-done.42, bf16[808,768]{1,0:T(8,128)(2,1)S(1)} %copy-done.13, bf16[768,768]{1,0:T(8,128)(2,1)S(1)} %copy-done), kind=kOutput, calls=%fused_computation.2 | convolution fusion | flops 999695616 | bytes 8632320 | tf_op jit(solution)/shard_map/dot_general | solution.py:99
  156.0 28.6 %fusion.2 = bf16[208,768]{1,0:T(8,128)(2,1)S(1)} fusion(bf16[808,768]{1,0:T(8,128)(2,1)} %convolution_convert_fusion), kind=kCustom, calls=%all-reduce-scatter.2 | all-reduce-scatter fusion | flops 638977 | bytes 1561088
  194.0 5.2 %collective-permute-done = bf16[1,202,768]{2,1,0:T(8,128)(2,1)} collective-permute-done((bf16[1,202,768]{2,1,0:T(8,128)(2,1)S(1)}, bf16[1,202,768]{2,1,0:T(8,128)(2,1)}, u32[]{:S(2)}, u32[]{:S(2)}) %collective-permute-start) | collective-permute-done | bytes 310304 | tf_op jit(solution)/shard_map/ppermute | solution.py:22
  204.0 25.6 %collective-permute-done.1 = bf16[2,202,768]{2,0,1:T(2,128)(2,1)} collective-permute-done((bf16[2,202,768]{2,0,1:T(2,128)(2,1)}, bf16[2,202,768]{2,0,1:T(2,128)(2,1)}, u32[]{:S(2)}, u32[]{:S(2)}) %collective-permute-start.1) | collective-permute-done | bytes 620576 | tf_op jit(solution)/shard_map/ppermute | solution.py:22
  233.2 2.7 reshape.156
  235.8 2.9 convolution_bitcast_fusion
  238.9 2.9 multiply_convert_fusion
  242.8 2.9 fusion.118
  246.5 4.7 %fusion.117 = f32[768,768]{1,0:T(8,128)} fusion(bf16[808,768]{1,0:T(8,128)(2,1)} %reshape.161, bf16[808,768]{1,0:T(8,128)(2,1)} %copy-done.50), kind=kOutput, calls=%fused_computation.202 | convolution fusion | flops 953155584 | bytes 4841472 | tf_op jit(solution)/shard_map/dot_general | solution.py:105
  271.6 2.8 fusion.116
  274.4 3.6 convolution_convert_fusion.1
  280.2 47.6 %fusion.110 = (bf16[208,768]{1,0:T(8,128)(2,1)S(1)}, bf16[208,768]{1,0:T(8,128)(2,1)S(1)}) fusion(bf16[808,768]{1,0:T(8,128)(2,1)} %convolution_convert_fusion.1, bf16[808,768]{1,0:T(8,128)(2,1)} %convolution_convert_fusion.3), kind=kCustom, calls=%all-reduce-scatter.4 | all-reduce-scatter fusion | flops 1277953 | bytes 3121664
  329.8 3.3 collective-permute-start.3
  333.2 13.5 %all-reduce.16 = (f32[576]{0:T(1024)}, f32[768]{0:T(1024)}) all-reduce(f32[576]{0:T(1024)S(1)} %reduce_sum.181, f32[768]{0:T(1024)S(1)} %copy-done.44), channel_id=1, replica_groups=mesh['dp'=8,'mp'=4] {'dp'}, use_global_device_ids=true, to_apply=%region_20.21 | all-reduce | flops 1344 | bytes 10752 | tf_op jit(solution)/shard_map/psum | solution.py:221
  349.4 38.2 %all-reduce.15 = (f32[768]{0:T(1024)}, f32[768]{0:T(1024)}, f32[768]{0:T(1024)}, f32[768]{0:T(1024)}, f32[768]{0:T(1024)}, /*index=5*/f32[768]{0:T(1024)}) all-reduce(f32[768]{0:T(1024)S(1)} %get-tuple-element.16, f32[768]{0:T(1024)S(1)} %get-tuple-element.21, ...), channel_id=1, replica_groups=mesh['dp'=8,'mp'=4] {'dp','mp'}, use_global_device_ids=true, to_apply=%region_15.16 | all-reduce | flops 4608 | bytes 36864 | tf_op jit(solution)/shard_map/psum | solution.py:222
  391.4 18.7 %reduce-scatter.15.cloned.1.call-done = f32[96,576]{1,0:T(8,128)} async-done(((f32[768,576]{1,0:T(8,128)}), f32[96,576]{1,0:T(8,128)}) %reduce-scatter.15.cloned.1.call-update) | async-done | bytes 221200 | tf_op jit(solution)/shard_map/reduce_scatter | solution.py:216
  (218 shorter events, 80.4 us)
Async XLA Ops:
  7.2 137.1 %copy-start = (bf16[768,768]{1,0:T(8,128)(2,1)S(1)}, bf16[768,768]{1,0:T(8,128)(2,1)}, u32[]{:S(2)}) copy-start(bf16[768,768]{1,0:T(8,128)(2,1)} %param.29) | copy-start | bytes 3538948
  7.2 39.3 %all-gather.7.cloned.1.call-start = ((), (), s32[]{:S(2)}) async-start(), calls=%async_computation.7 | async-start | bytes 1597440 | tf_op jit(solution)/shard_map/all_gather | solution.py:141
  9.7 39.5 %copy-start.48 = (f32[576]{0:T(1024)S(1)}, f32[576]{0:T(1024)}, u32[]{:S(2)}) copy-start(f32[576]{0:T(1024)} %param.21) | copy-start | bytes 6916
  11.7 94.1 %all-gather.11.cloned.1.call-start = ((), (), s32[]{:S(2)}) async-start(), calls=%async_computation.9 | async-start | bytes 1597440 | tf_op jit(solution)/shard_map/all_gather | solution.py:182
  12.4 126.2 %all-gather.9.cloned.1.call-start = ((), (), s32[]{:S(2)}) async-start(), calls=%async_computation.8 | async-start | bytes 1597440 | tf_op jit(solution)/shard_map/all_gather | solution.py:166
  13.3 45.8 %copy-start.31 = (f32[808]{0:T(1024)}, f32[808]{0:T(1024)S(1)}, u32[]{:S(2)}) copy-start(f32[808]{0:T(1024)S(1)} %reshape.157) | copy-start | bytes 9700
  64.8 39.0 %copy-start.1 = (bf16[202,768]{1,0:T(8,128)(2,1)S(1)}, bf16[202,768]{1,0:T(8,128)(2,1)}, u32[]{:S(2)}) copy-start(bf16[202,768]{1,0:T(8,128)(2,1)} %param.16) | copy-start | bytes 930820
  65.1 39.3 %copy-start.29 = (f32[768]{0:T(1024)S(1)}, f32[768]{0:T(1024)}, u32[]{:S(2)}) copy-start(f32[768]{0:T(1024)} %param.25) | copy-start | bytes 9220
  65.1 39.3 %copy-start.41 = (f32[768]{0:T(1024)S(1)}, f32[768]{0:T(1024)}, u32[]{:S(2)}) copy-start(f32[768]{0:T(1024)} %param.26) | copy-start | bytes 9220
  100.5 2.9 collective-permute-start.2
  104.1 84.1 %copy-start.35 = (f32[202]{0:T(256)}, f32[202]{0:T(256)S(1)}, u32[]{:S(2)}) copy-start(f32[202]{0:T(256)S(1)} %broadcast_multiply_fusion.6) | copy-start | bytes 2428
  104.4 83.8 %copy-start.40 = (f32[202]{0:T(256)}, f32[202]{0:T(256)S(1)}, u32[]{:S(2)}) copy-start(f32[202]{0:T(256)S(1)} %add_rsqrt_fusion) | copy-start | bytes 2428
  105.5 284.3 %reduce-scatter.21.cloned.1.call-start = ((), (), s32[]{:S(2)}) async-start(), calls=%async_computation.10 | async-start | bytes 884736
  184.6 3.2 collective-permute-start.4
  191.6 7.6 %collective-permute-start = (bf16[1,202,768]{2,1,0:T(8,128)(2,1)S(1)}, bf16[1,202,768]{2,1,0:T(8,128)(2,1)}, u32[]{:S(2)}, u32[]{:S(2)}) collective-permute-start(bf16[1,202,768]{2,1,0:T(8,128)(2,1)S(1)} %convert_bitcast_fusion), channel_id=1, source_target_pairs={{0,1},{1,0},{2,3},{3,2},{4,5},{5,4},{6,7},{7,6},{8,9},{9,8},{10,11... | collective-permute-start | bytes 930824 | tf_op jit(solution)/shard_map/ppermute | solution.py:22
  202.4 27.2 %collective-permute-start.1 = (bf16[2,202,768]{2,0,1:T(2,128)(2,1)}, bf16[2,202,768]{2,0,1:T(2,128)(2,1)}, u32[]{:S(2)}, u32[]{:S(2)}) collective-permute-start(bf16[2,202,768]{2,0,1:T(2,128)(2,1)} %copy.77), channel_id=1, source_target_pairs={{0,2},{1,3},{2,0},{3,1},{4,6},{5,7},{6,4},{7,5},{8,10},{9,11},{10,... | collective-permute-start | bytes 1861640 | tf_op jit(solution)/shard_map/ppermute | solution.py:22
  238.8 152.6 %reduce-scatter.19.cloned.1.call-start = ((), (), s32[]{:S(2)}) async-start(), calls=%async_computation.6 | async-start | bytes 2654208 | tf_op jit(solution)/shard_map/reduce_scatter | solution.py:219
  245.7 145.7 %reduce-scatter.17.cloned.1.call-start = ((), (), s32[]{:S(2)}) async-start(), calls=%async_computation.5 | async-start | bytes 2654208 | tf_op jit(solution)/shard_map/reduce_scatter | solution.py:218
  251.2 158.9 %reduce-scatter.15.cloned.1.call-start = ((), (), s32[]{:S(2)}) async-start(), calls=%async_computation.4 | async-start | bytes 2211840 | tf_op jit(solution)/shard_map/reduce_scatter | solution.py:216
  280.2 53.0 %copy-start.44 = (f32[768]{0:T(1024)S(1)}, f32[768]{0:T(1024)}, u32[]{:S(2)}) copy-start(f32[768]{0:T(1024)} %get-tuple-element.34) | copy-start | bytes 9220
  280.2 68.0 %copy-start.30 = (f32[768]{0:T(1024)S(1)}, f32[768]{0:T(1024)}, u32[]{:S(2)}) copy-start(f32[768]{0:T(1024)} %param.18) | copy-start | bytes 9220
  280.2 68.0 %copy-start.34 = (f32[202]{0:T(256)S(1)}, f32[202]{0:T(256)}, u32[]{:S(2)}) copy-start(f32[202]{0:T(256)} %copy-done.33) | copy-start | bytes 2428
  327.9 18.8 %collective-permute-start.5 = (bf16[18,768]{1,0:T(8,128)(2,1)S(1)}, bf16[18,768]{1,0:T(8,128)(2,1)S(1)}, u32[]{:S(2)}, u32[]{:S(2)}) collective-permute-start(bf16[18,768]{1,0:T(8,128)(2,1)S(1)} %slice.39), channel_id=1, source_target_pairs={{0,1},{1,2},{2,3},{4,5},{5,6},{6,7},{8,9},{9,10},{10,11},{12,13},{... | collective-permute-start | bytes 82952
  329.8 17.2 %collective-permute-start.3 = (bf16[18,768]{1,0:T(8,128)(2,1)}, bf16[18,768]{1,0:T(8,128)(2,1)}, u32[]{:S(2)}, u32[]{:S(2)}) collective-permute-start(bf16[18,768]{1,0:T(8,128)(2,1)} %slice.37), channel_id=1, source_target_pairs={{0,1},{1,2},{2,3},{4,5},{5,6},{6,7},{8,9},{9,10},{10,11},{12,13},{... | collective-permute-start | bytes 82952
  (40 other events, 198.4 us)
Sparse Core Ops, SparseCore 0:
  11.8 34.6 all-gather.6
  48.0 36.9 all-gather.10
  105.6 33.0 all-gather.8
  238.9 34.4 reduce-scatter.20
  277.2 42.3 reduce-scatter.18
  323.3 42.6 reduce-scatter.16
  370.0 40.1 reduce-scatter.14
